TPU v7x, 1024 devices: a whole 8x8x8 slice. The times are simulated.
1024 devices in a mesh: comp: 2 (over core), lat: 32 (over x, z_hi), lon: 16 (over z_lo, y).
Axes of the slice: x: 8, y: 8, z: 8 (z_hi: 4, z_lo: 2; z = z_hi * 2 + z_lo), core: 2. Of those that a mesh axis runs over, the one named last changes fastest.
Arguments:
- state: float32 [2, 80, 256, 2048], P('comp', None, 'lat', 'lon')
- mixing: float32 [2, 80, 80], P('comp')
- diffusivity: float32 [2, 80], P('comp'), may hold values from 0.22 to 0.25
- weights: float32 [2, 64], P('comp'), may hold values from 0.25 to 1
- links: int32 [2, 32, 16, 4, 32], P('comp', 'lat', 'lon'), may hold values from 0 to 63, as said below
- land: int32 [256, 16], P('lat', 'lon'), may hold values 0 or 1
- depth: int32 [256, 16], P('lat', 'lon'), may hold values from 79 to 80
Outputs:
- advanced: float32 [2, 80, 256, 2048], P('comp', None, 'lat', 'lon')
Inputs may be any that keep to these rules, and one draw needn't show every extreme that they name: Entries are source row below 8, destination lon index below 16, destination row below 8, weight index below 64. A device's links come in 8 consecutive groups of 4, each group with one destination, distinct within the device; in every latitude row of a section, the first group of every device has the same destination.
All inputs are finite; a program needn't handle non-finite values. No bound on the sum of `land` on one device may be relied on, other than what follows from the above.
Results may differ from a plain program's by a relative error of at most 0.0003.
Values sent between devices are 32-bit elements; how exact they have to be, the bound alone decides.
A program may use at most 32 MiB of HBM per device.

v0:
```python
import jax
import jax.numpy as jnp
from jax import lax
from jax.sharding import PartitionSpec as P

STEPS = 4
CAP = 4


coupling_rate = 0.5


def swapped(value, axis, bit):
    mask = 2**bit
    pairs = [(source, source ^ mask) for source in range(lax.axis_size(axis))]
    return lax.ppermute(value, axis, pairs)


def padded_2(shard, sides, width):
    for axis, dim in sides:
        size, length = (lax.axis_size(axis), shard.shape[dim])
        up = [(i, (i + 1) % size) for i in range(size)]
        down = [(j, i) for i, j in up]
        last = lax.slice_in_dim(shard, length - width, length, axis=dim)
        first = lax.slice_in_dim(shard, 0, width, axis=dim)
        before = lax.ppermute(last, axis, up)
        after = lax.ppermute(first, axis, down)
        shard = jnp.concatenate([before, shard, after], axis=dim)
    return shard


def advance(padded, diffuse, flux_one, active, mix_mat):
    middle = padded[:, 1:-1, 1:-1]
    neighbours = (
        padded[:, 2:, 1:-1] + padded[:, :-2, 1:-1] + padded[:, 1:-1, 2:] + padded[:, 1:-1, :-2]
    )
    moved = middle + diffuse * (neighbours - 4.0 * middle)
    moved = moved.at[0].add(flux_one)
    levels = middle.shape[0]
    mixed = jnp.dot(
        mix_mat,
        (moved * active).reshape(levels, -1),
        precision=lax.Precision.HIGHEST,
        preferred_element_type=jnp.float32,
    ).reshape(middle.shape)
    return active * mixed + (1.0 - active) * middle


def on_device(state, mixing, diffusivity, weights, links, land, depth):
    tracer = state[0]
    mix_mat = mixing[0]
    diffuse = diffusivity[0][:, None, None]
    levels, row_count, cell_count = tracer.shape
    ocean_flag = lax.axis_index("comp") == 1
    sea_cells = jnp.broadcast_to(land.astype(jnp.float32), (row_count, cell_count))
    deep_cells = jnp.broadcast_to((land * depth).astype(jnp.float32), (row_count, cell_count))
    level_ids = jnp.arange(levels, dtype=jnp.float32)[:, None, None]
    surface = tracer[0]
    link_table = links.reshape(4, -1)
    sources = link_table[0]
    targets = link_table[1]
    dest_rows = link_table[2]
    weight_ids = link_table[3]
    row_ids = jnp.arange(row_count, dtype=jnp.int32)
    picker = (sources[:, None] == row_ids[None, :]).astype(jnp.float32)
    picked = jnp.dot(
        picker, surface, precision=lax.Precision.HIGHEST, preferred_element_type=jnp.float32
    )
    table = weights[0]
    weight_link = jnp.sum(
        jnp.where(
            weight_ids[:, None] == jnp.arange(table.shape[0], dtype=jnp.int32)[None, :],
            table[None, :],
            0.0,
        ),
        axis=1,
    )
    values = picked * weight_link[:, None]
    lon_count = lax.axis_size("lon")
    group_dest = targets.reshape(-1, CAP)[:, 0]
    placing = (jnp.arange(lon_count, dtype=jnp.int32)[:, None] == group_dest[None, :]).astype(
        jnp.float32
    )
    slots_out = jnp.einsum(
        "ng,gkc->nkc", placing, values.reshape(-1, CAP, cell_count), precision=lax.Precision.HIGHEST
    )
    link_meta = jnp.stack([weight_link, dest_rows.astype(jnp.float32)], axis=-1).reshape(-1, CAP, 2)
    meta_out = jnp.einsum("ng,gke->nke", placing, link_meta, precision=lax.Precision.HIGHEST)
    crossed, cross_meta = swapped((slots_out, meta_out), "comp", 0)
    received, recv_meta = (
        lax.all_to_all(crossed, "lon", split_axis=0, concat_axis=0, tiled=True),
        lax.all_to_all(cross_meta, "lon", split_axis=0, concat_axis=0, tiled=True),
    )
    recv_rows = recv_meta[..., 1].reshape(-1)
    recv_wts = recv_meta[..., 0].reshape(-1)
    select = (row_ids.astype(jnp.float32)[:, None] == recv_rows[None, :]).astype(jnp.float32)
    accum = jnp.dot(
        select,
        received.reshape(-1, cell_count),
        precision=lax.Precision.HIGHEST,
        preferred_element_type=jnp.float32,
    )
    totals = jnp.dot(
        select,
        recv_wts[:, None],
        precision=lax.Precision.HIGHEST,
        preferred_element_type=jnp.float32,
    )
    imported = accum / jnp.maximum(totals, 1.0)
    flux_field = coupling_rate * sea_cells * (imported - surface)
    lat_pos = lax.axis_index("lat")
    lat_count = lax.axis_size("lat")
    ocean_part = (level_ids < deep_cells[None]).astype(jnp.float32)
    active = jnp.where(ocean_flag, ocean_part, jnp.ones_like(ocean_part))
    padded_ids = jnp.arange(row_count + 2, dtype=jnp.int32)
    row_keep = jnp.where(padded_ids == 0, (lat_pos > 0).astype(jnp.float32), 1.0)
    row_keep = jnp.where(
        padded_ids == row_count + 1, (lat_pos < lat_count - 1).astype(jnp.float32), row_keep
    )
    for step in range(STEPS):
        padded = padded_2(tracer, (("lat", 1), ("lon", 2)), 1)
        padded = padded * row_keep[None, :, None]
        tracer = advance(padded, diffuse, flux_field, active, mix_mat)
    return tracer[None]


def solution(mesh):
    in_specs = (
        P("comp", None, "lat", "lon"),
        P("comp", None, None),
        P("comp", None),
        P("comp", None),
        P("comp", "lat", "lon", None, None),
        P("lat", "lon"),
        P("lat", "lon"),
    )
    out_specs = P("comp", None, "lat", "lon")
    return jax.shard_map(
        on_device, mesh=mesh, in_specs=in_specs, out_specs=out_specs, check_vma=False
    )
```

profile of v0, /device:TPU:14, one launch (start us, length us, event | category | flops | bytes accessed | tf_op | source)
XLA Modules:
  0.0 146.5 jit_solution(3418808803410146887)
XLA Ops:
  0.0 0.7 convert_reduce_fusion
  0.7 0.8 slice_reduce_fusion.3
  1.9 0.8 select_reduce_fusion
  3.1 1.9 %collective-permute-start.4 = (f32[16,4,2]{0,1,2:T(4,128)S(1)}, f32[16,4,2]{0,1,2:T(4,128)S(1)}, u32[]{:S(2)}, u32[]{:S(2)}) collective-permute-start(f32[16,4,2]{0,1,2:T(4,128)S(1)} %fusion.46), channel_id=1, source_target_pairs={{0,512},{512,0},{1,513},{513,1},{2,514},{514,2},{3,515},{515,3},{4... | collective-permute-start | bytes 1544 | tf_op jit(solution)/shard_map/ppermute | solution.py:16
  5.0 0.9 convolution_multiply_fusion
  5.9 0.3 fusion.37
  6.2 2.4 %collective-permute-start.5 = (f32[16,4,128]{2,0,1:T(8,128)S(1)}, f32[16,4,128]{2,0,1:T(8,128)S(1)}, u32[]{:S(2)}, u32[]{:S(2)}) collective-permute-start(f32[16,4,128]{2,0,1:T(8,128)S(1)} %fusion.37), channel_id=1, source_target_pairs={{0,512},{512,0},{1,513},{513,1},{2,514},{514,2},{3,515},{515,3},{4... | collective-permute-start | bytes 98312 | tf_op jit(solution)/shard_map/ppermute | solution.py:16
  8.6 1.1 fusion.69
  9.7 7.9 %collective-permute-start = (f32[80,1,128]{2,1,0:T(1,128)S(1)}, f32[80,1,128]{2,1,0:T(1,128)S(1)}, u32[]{:S(2)}, u32[]{:S(2)}) collective-permute-start(f32[80,1,128]{2,1,0:T(1,128)S(1)} %get-tuple-element.69), channel_id=1, source_target_pairs={{0,16},{16,32},{32,48},{48,64},{64,80},{80,96},{96,112},{112,128},... | collective-permute-start | bytes 122888 | tf_op jit(solution)/shard_map/ppermute | solution.py:26
  17.6 11.3 %collective-permute-start.1 = (f32[80,1,128]{2,1,0:T(1,128)S(1)}, f32[80,1,128]{2,1,0:T(1,128)S(1)}, u32[]{:S(2)}, u32[]{:S(2)}) collective-permute-start(f32[80,1,128]{2,1,0:T(1,128)S(1)} %get-tuple-element.70), channel_id=1, source_target_pairs={{16,0},{32,16},{48,32},{64,48},{80,64},{96,80},{112,96},{128,112},... | collective-permute-start | bytes 122888 | tf_op jit(solution)/shard_map/ppermute | solution.py:27
  28.9 0.7 multiply_bitcast_fusion
  29.6 0.7 convert_bitcast_fusion
  30.3 0.7 copy.46
  31.0 9.5 %all-to-all-start = ((f32[16,4,2]{1,2,0:T(2,128)}), f32[16,4,2]{1,2,0:T(2,128)S(1)}, u32[]{:S(2)}, u32[]{:S(2)}) async-start(f32[16,4,2]{1,2,0:T(2,128)} %copy.46), calls=%async_computation | async-start | bytes 32768 | tf_op jit(solution)/shard_map/all_to_all | solution.py:92
  40.5 8.5 %all-to-all-done = f32[16,4,2]{1,2,0:T(2,128)S(1)} async-done(((f32[16,4,2]{1,2,0:T(2,128)}), f32[16,4,2]{1,2,0:T(2,128)S(1)}, u32[]{:S(2)}, u32[]{:S(2)}) %all-to-all-start) | async-done | bytes 544 | tf_op jit(solution)/shard_map/all_to_all | solution.py:92
  49.2 1.1 pad_maximum_fusion
  50.3 0.2 fusion.65
  51.0 2.6 %collective-permute-start.3 = (f32[80,10,1]{0,2,1:T(1,128)S(1)}, f32[80,10,1]{0,2,1:T(1,128)S(1)}, u32[]{:S(2)}, u32[]{:S(2)}) collective-permute-start(f32[80,10,1]{0,2,1:T(1,128)S(1)} %copy.41), channel_id=1, source_target_pairs={{1,0},{2,1},{3,2},{4,3},{5,4},{6,5},{7,6},{8,7},{9,8},{10,9},{11,1... | collective-permute-start | bytes 9608 | tf_op jit(solution)/shard_map/ppermute | solution.py:27
  53.6 3.2 %collective-permute-start.2 = (f32[80,10,1]{0,2,1:T(1,128)S(1)}, f32[80,10,1]{0,2,1:T(1,128)S(1)}, u32[]{:S(2)}, u32[]{:S(2)}) collective-permute-start(f32[80,10,1]{0,2,1:T(1,128)S(1)} %copy.40), channel_id=1, source_target_pairs={{0,1},{1,2},{2,3},{3,4},{4,5},{5,6},{6,7},{7,8},{8,9},{9,10},{10,1... | collective-permute-start | bytes 9608 | tf_op jit(solution)/shard_map/ppermute | solution.py:26
  57.0 0.6 copy.48
  57.7 4.2 %all-to-all-start.1 = ((f32[16,4,128]{2,1,0:T(4,128)}), f32[16,4,128]{2,1,0:T(4,128)S(1)}, u32[]{:S(2)}, u32[]{:S(2)}) async-start(f32[16,4,128]{2,1,0:T(4,128)} %copy.48), calls=%async_computation.1 | async-start | bytes 65536 | tf_op jit(solution)/shard_map/all_to_all | solution.py:91
  61.9 0.4 copy.42
  62.3 0.4 copy.43
  62.7 0.9 maximum_multiply_fusion
  63.6 0.5 fusion.27
  64.1 6.3 %all-to-all-done.1 = f32[16,4,128]{2,1,0:T(4,128)S(1)} async-done(((f32[16,4,128]{2,1,0:T(4,128)}), f32[16,4,128]{2,1,0:T(4,128)S(1)}, u32[]{:S(2)}, u32[]{:S(2)}) %all-to-all-start.1) | async-done | bytes 32800 | tf_op jit(solution)/shard_map/all_to_all | solution.py:91
  70.7 0.5 convolution_bitcast_fusion.3
  71.5 1.9 %collective-permute-start.6 = (f32[80,1,128]{2,1,0:T(1,128)S(1)}, f32[80,1,128]{2,1,0:T(1,128)S(1)}, u32[]{:S(2)}, u32[]{:S(2)}) collective-permute-start(f32[80,1,128]{2,1,0:T(1,128)S(1)} %get-tuple-element.67), channel_id=1, source_target_pairs={{0,16},{16,32},{32,48},{48,64},{64,80},{80,96},{96,112},{112,128},... | collective-permute-start | bytes 122888 | tf_op jit(solution)/shard_map/ppermute | solution.py:26
  73.4 6.9 %collective-permute-start.7 = (f32[80,1,128]{2,1,0:T(1,128)S(1)}, f32[80,1,128]{2,1,0:T(1,128)S(1)}, u32[]{:S(2)}, u32[]{:S(2)}) collective-permute-start(f32[80,1,128]{2,1,0:T(1,128)S(1)} %get-tuple-element.68), channel_id=1, source_target_pairs={{16,0},{32,16},{48,32},{64,48},{80,64},{96,80},{112,96},{128,112},... | collective-permute-start | bytes 122888 | tf_op jit(solution)/shard_map/ppermute | solution.py:27
  80.4 1.6 %collective-permute-done.7 = f32[80,1,128]{2,1,0:T(1,128)S(1)} collective-permute-done((f32[80,1,128]{2,1,0:T(1,128)S(1)}, f32[80,1,128]{2,1,0:T(1,128)S(1)}, u32[]{:S(2)}, u32[]{:S(2)}) %collective-permute-start.7) | collective-permute-done | bytes 40992 | tf_op jit(solution)/shard_map/ppermute | solution.py:27
  82.1 0.2 fusion.64
  82.6 2.6 %collective-permute-start.8 = (f32[80,10,1]{0,2,1:T(1,128)S(1)}, f32[80,10,1]{0,2,1:T(1,128)S(1)}, u32[]{:S(2)}, u32[]{:S(2)}) collective-permute-start(f32[80,10,1]{0,2,1:T(1,128)S(1)} %copy.49), channel_id=1, source_target_pairs={{0,1},{1,2},{2,3},{3,4},{4,5},{5,6},{6,7},{7,8},{8,9},{9,10},{10,1... | collective-permute-start | bytes 9608 | tf_op jit(solution)/shard_map/ppermute | solution.py:26
  85.4 5.4 %collective-permute-start.9 = (f32[80,10,1]{0,2,1:T(1,128)S(1)}, f32[80,10,1]{0,2,1:T(1,128)S(1)}, u32[]{:S(2)}, u32[]{:S(2)}) collective-permute-start(f32[80,10,1]{0,2,1:T(1,128)S(1)} %copy.50), channel_id=1, source_target_pairs={{1,0},{2,1},{3,2},{4,3},{5,4},{6,5},{7,6},{8,7},{9,8},{10,9},{11,1... | collective-permute-start | bytes 9608 | tf_op jit(solution)/shard_map/ppermute | solution.py:27
  90.8 0.4 copy.51
  91.1 0.9 collective-permute-done.9
  92.1 0.4 copy.52
  92.4 0.9 maximum_multiply_fusion.1
  93.4 0.5 fusion.24
  94.0 0.5 convolution_bitcast_fusion.2
  94.8 3.8 %collective-permute-start.10 = (f32[80,1,128]{2,1,0:T(1,128)S(1)}, f32[80,1,128]{2,1,0:T(1,128)S(1)}, u32[]{:S(2)}, u32[]{:S(2)}) collective-permute-start(f32[80,1,128]{2,1,0:T(1,128)S(1)} %get-tuple-element.65), channel_id=1, source_target_pairs={{0,16},{16,32},{32,48},{48,64},{64,80},{80,96},{96,112},{112,128},... | collective-permute-start | bytes 122888 | tf_op jit(solution)/shard_map/ppermute | solution.py:26
  98.6 5.7 %collective-permute-start.11 = (f32[80,1,128]{2,1,0:T(1,128)S(1)}, f32[80,1,128]{2,1,0:T(1,128)S(1)}, u32[]{:S(2)}, u32[]{:S(2)}) collective-permute-start(f32[80,1,128]{2,1,0:T(1,128)S(1)} %get-tuple-element.66), channel_id=1, source_target_pairs={{16,0},{32,16},{48,32},{64,48},{80,64},{96,80},{112,96},{128,112},... | collective-permute-start | bytes 122888 | tf_op jit(solution)/shard_map/ppermute | solution.py:27
  104.4 1.6 %collective-permute-done.11 = f32[80,1,128]{2,1,0:T(1,128)S(1)} collective-permute-done((f32[80,1,128]{2,1,0:T(1,128)S(1)}, f32[80,1,128]{2,1,0:T(1,128)S(1)}, u32[]{:S(2)}, u32[]{:S(2)}) %collective-permute-start.11) | collective-permute-done | bytes 40992 | tf_op jit(solution)/shard_map/ppermute | solution.py:27
  106.1 0.2 fusion.63
  106.6 1.9 %collective-permute-start.12 = (f32[80,10,1]{0,2,1:T(1,128)S(1)}, f32[80,10,1]{0,2,1:T(1,128)S(1)}, u32[]{:S(2)}, u32[]{:S(2)}) collective-permute-start(f32[80,10,1]{0,2,1:T(1,128)S(1)} %copy.53), channel_id=1, source_target_pairs={{0,1},{1,2},{2,3},{3,4},{4,5},{5,6},{6,7},{7,8},{8,9},{9,10},{10,1... | collective-permute-start | bytes 9608 | tf_op jit(solution)/shard_map/ppermute | solution.py:26
  108.7 6.5 %collective-permute-start.13 = (f32[80,10,1]{0,2,1:T(1,128)S(1)}, f32[80,10,1]{0,2,1:T(1,128)S(1)}, u32[]{:S(2)}, u32[]{:S(2)}) collective-permute-start(f32[80,10,1]{0,2,1:T(1,128)S(1)} %copy.54), channel_id=1, source_target_pairs={{1,0},{2,1},{3,2},{4,3},{5,4},{6,5},{7,6},{8,7},{9,8},{10,9},{11,1... | collective-permute-start | bytes 9608 | tf_op jit(solution)/shard_map/ppermute | solution.py:27
  115.2 0.4 copy.55
  115.6 0.8 collective-permute-done.13
  116.3 0.4 copy.56
  116.7 0.9 maximum_multiply_fusion.2
  117.6 0.5 fusion.21
  118.2 0.5 convolution_bitcast_fusion.1
  119.0 6.9 %collective-permute-start.14 = (f32[80,1,128]{2,1,0:T(1,128)S(1)}, f32[80,1,128]{2,1,0:T(1,128)S(1)}, u32[]{:S(2)}, u32[]{:S(2)}) collective-permute-start(f32[80,1,128]{2,1,0:T(1,128)S(1)} %get-tuple-element.63), channel_id=1, source_target_pairs={{0,16},{16,32},{32,48},{48,64},{64,80},{80,96},{96,112},{112,128},... | collective-permute-start | bytes 122888 | tf_op jit(solution)/shard_map/ppermute | solution.py:26
  125.9 2.4 %collective-permute-start.15 = (f32[80,1,128]{2,1,0:T(1,128)S(1)}, f32[80,1,128]{2,1,0:T(1,128)S(1)}, u32[]{:S(2)}, u32[]{:S(2)}) collective-permute-start(f32[80,1,128]{2,1,0:T(1,128)S(1)} %get-tuple-element.64), channel_id=1, source_target_pairs={{16,0},{32,16},{48,32},{64,48},{80,64},{96,80},{112,96},{128,112},... | collective-permute-start | bytes 122888 | tf_op jit(solution)/shard_map/ppermute | solution.py:27
  128.3 4.7 %collective-permute-done.15 = f32[80,1,128]{2,1,0:T(1,128)S(1)} collective-permute-done((f32[80,1,128]{2,1,0:T(1,128)S(1)}, f32[80,1,128]{2,1,0:T(1,128)S(1)}, u32[]{:S(2)}, u32[]{:S(2)}) %collective-permute-start.15) | collective-permute-done | bytes 40992 | tf_op jit(solution)/shard_map/ppermute | solution.py:27
  133.1 0.2 fusion.62
  133.6 1.9 %collective-permute-start.16 = (f32[80,10,1]{0,2,1:T(1,128)S(1)}, f32[80,10,1]{0,2,1:T(1,128)S(1)}, u32[]{:S(2)}, u32[]{:S(2)}) collective-permute-start(f32[80,10,1]{0,2,1:T(1,128)S(1)} %copy.57), channel_id=1, source_target_pairs={{0,1},{1,2},{2,3},{3,4},{4,5},{5,6},{6,7},{7,8},{8,9},{9,10},{10,1... | collective-permute-start | bytes 9608 | tf_op jit(solution)/shard_map/ppermute | solution.py:26
  135.7 6.1 %collective-permute-start.17 = (f32[80,10,1]{0,2,1:T(1,128)S(1)}, f32[80,10,1]{0,2,1:T(1,128)S(1)}, u32[]{:S(2)}, u32[]{:S(2)}) collective-permute-start(f32[80,10,1]{0,2,1:T(1,128)S(1)} %copy.58), channel_id=1, source_target_pairs={{1,0},{2,1},{3,2},{4,3},{5,4},{6,5},{7,6},{8,7},{9,8},{10,9},{11,1... | collective-permute-start | bytes 9608 | tf_op jit(solution)/shard_map/ppermute | solution.py:27
  141.8 0.4 copy.59
  142.2 0.9 collective-permute-done.17
  143.1 0.4 copy.60
  143.5 0.9 maximum_multiply_fusion.3
  144.4 0.5 fusion.18
  145.0 0.5 convolution_bitcast_fusion
  145.6 0.9 fusion.4
  (60 shorter events, 5.0 us)
Async XLA Ops:
  0.0 70.7 %copy-start = (f32[1,80,80]{2,1,0:T(8,128)S(1)}, f32[1,80,80]{2,1,0:T(8,128)}, u32[]{:S(2)}) copy-start(f32[1,80,80]{2,1,0:T(8,128)} %param.16) | copy-start | bytes 76804
  3.1 27.2 %collective-permute-start.4 = (f32[16,4,2]{0,1,2:T(4,128)S(1)}, f32[16,4,2]{0,1,2:T(4,128)S(1)}, u32[]{:S(2)}, u32[]{:S(2)}) collective-permute-start(f32[16,4,2]{0,1,2:T(4,128)S(1)} %fusion.46), channel_id=1, source_target_pairs={{0,512},{512,0},{1,513},{513,1},{2,514},{514,2},{3,515},{515,3},{4... | collective-permute-start | bytes 1544 | tf_op jit(solution)/shard_map/ppermute | solution.py:16
  6.2 50.9 %collective-permute-start.5 = (f32[16,4,128]{2,0,1:T(8,128)S(1)}, f32[16,4,128]{2,0,1:T(8,128)S(1)}, u32[]{:S(2)}, u32[]{:S(2)}) collective-permute-start(f32[16,4,128]{2,0,1:T(8,128)S(1)} %fusion.37), channel_id=1, source_target_pairs={{0,512},{512,0},{1,513},{513,1},{2,514},{514,2},{3,515},{515,3},{4... | collective-permute-start | bytes 98312 | tf_op jit(solution)/shard_map/ppermute | solution.py:16
  9.7 39.5 %collective-permute-start = (f32[80,1,128]{2,1,0:T(1,128)S(1)}, f32[80,1,128]{2,1,0:T(1,128)S(1)}, u32[]{:S(2)}, u32[]{:S(2)}) collective-permute-start(f32[80,1,128]{2,1,0:T(1,128)S(1)} %get-tuple-element.69), channel_id=1, source_target_pairs={{0,16},{16,32},{32,48},{48,64},{64,80},{80,96},{96,112},{112,128},... | collective-permute-start | bytes 122888 | tf_op jit(solution)/shard_map/ppermute | solution.py:26
  17.6 31.5 %collective-permute-start.1 = (f32[80,1,128]{2,1,0:T(1,128)S(1)}, f32[80,1,128]{2,1,0:T(1,128)S(1)}, u32[]{:S(2)}, u32[]{:S(2)}) collective-permute-start(f32[80,1,128]{2,1,0:T(1,128)S(1)} %get-tuple-element.70), channel_id=1, source_target_pairs={{16,0},{32,16},{48,32},{64,48},{80,64},{96,80},{112,96},{128,112},... | collective-permute-start | bytes 122888 | tf_op jit(solution)/shard_map/ppermute | solution.py:27
  31.0 18.0 %all-to-all-start = ((f32[16,4,2]{1,2,0:T(2,128)}), f32[16,4,2]{1,2,0:T(2,128)S(1)}, u32[]{:S(2)}, u32[]{:S(2)}) async-start(f32[16,4,2]{1,2,0:T(2,128)} %copy.46), calls=%async_computation | async-start | bytes 32768 | tf_op jit(solution)/shard_map/all_to_all | solution.py:92
  50.5 12.1 %copy-start.1 = (f32[1,80,8,128]{3,2,1,0:T(8,128)S(1)}, f32[1,80,8,128]{3,2,1,0:T(8,128)}, u32[]{:S(2)}) copy-start(f32[1,80,8,128]{3,2,1,0:T(8,128)} %param.15) | copy-start | bytes 983044
  51.0 11.3 %collective-permute-start.3 = (f32[80,10,1]{0,2,1:T(1,128)S(1)}, f32[80,10,1]{0,2,1:T(1,128)S(1)}, u32[]{:S(2)}, u32[]{:S(2)}) collective-permute-start(f32[80,10,1]{0,2,1:T(1,128)S(1)} %copy.41), channel_id=1, source_target_pairs={{1,0},{2,1},{3,2},{4,3},{5,4},{6,5},{7,6},{8,7},{9,8},{10,9},{11,1... | collective-permute-start | bytes 9608 | tf_op jit(solution)/shard_map/ppermute | solution.py:27
  53.6 8.3 %collective-permute-start.2 = (f32[80,10,1]{0,2,1:T(1,128)S(1)}, f32[80,10,1]{0,2,1:T(1,128)S(1)}, u32[]{:S(2)}, u32[]{:S(2)}) collective-permute-start(f32[80,10,1]{0,2,1:T(1,128)S(1)} %copy.40), channel_id=1, source_target_pairs={{0,1},{1,2},{2,3},{3,4},{4,5},{5,6},{6,7},{7,8},{8,9},{9,10},{10,1... | collective-permute-start | bytes 9608 | tf_op jit(solution)/shard_map/ppermute | solution.py:26
  57.7 12.7 %all-to-all-start.1 = ((f32[16,4,128]{2,1,0:T(4,128)}), f32[16,4,128]{2,1,0:T(4,128)S(1)}, u32[]{:S(2)}, u32[]{:S(2)}) async-start(f32[16,4,128]{2,1,0:T(4,128)} %copy.48), calls=%async_computation.1 | async-start | bytes 65536 | tf_op jit(solution)/shard_map/all_to_all | solution.py:91
  62.6 0.9 copy-start.2
  71.5 8.9 %collective-permute-start.6 = (f32[80,1,128]{2,1,0:T(1,128)S(1)}, f32[80,1,128]{2,1,0:T(1,128)S(1)}, u32[]{:S(2)}, u32[]{:S(2)}) collective-permute-start(f32[80,1,128]{2,1,0:T(1,128)S(1)} %get-tuple-element.67), channel_id=1, source_target_pairs={{0,16},{16,32},{32,48},{48,64},{64,80},{80,96},{96,112},{112,128},... | collective-permute-start | bytes 122888 | tf_op jit(solution)/shard_map/ppermute | solution.py:26
  73.4 8.6 %collective-permute-start.7 = (f32[80,1,128]{2,1,0:T(1,128)S(1)}, f32[80,1,128]{2,1,0:T(1,128)S(1)}, u32[]{:S(2)}, u32[]{:S(2)}) collective-permute-start(f32[80,1,128]{2,1,0:T(1,128)S(1)} %get-tuple-element.68), channel_id=1, source_target_pairs={{16,0},{32,16},{48,32},{64,48},{80,64},{96,80},{112,96},{128,112},... | collective-permute-start | bytes 122888 | tf_op jit(solution)/shard_map/ppermute | solution.py:27
  82.6 8.2 %collective-permute-start.8 = (f32[80,10,1]{0,2,1:T(1,128)S(1)}, f32[80,10,1]{0,2,1:T(1,128)S(1)}, u32[]{:S(2)}, u32[]{:S(2)}) collective-permute-start(f32[80,10,1]{0,2,1:T(1,128)S(1)} %copy.49), channel_id=1, source_target_pairs={{0,1},{1,2},{2,3},{3,4},{4,5},{5,6},{6,7},{7,8},{8,9},{9,10},{10,1... | collective-permute-start | bytes 9608 | tf_op jit(solution)/shard_map/ppermute | solution.py:26
  85.4 6.7 %collective-permute-start.9 = (f32[80,10,1]{0,2,1:T(1,128)S(1)}, f32[80,10,1]{0,2,1:T(1,128)S(1)}, u32[]{:S(2)}, u32[]{:S(2)}) collective-permute-start(f32[80,10,1]{0,2,1:T(1,128)S(1)} %copy.50), channel_id=1, source_target_pairs={{1,0},{2,1},{3,2},{4,3},{5,4},{6,5},{7,6},{8,7},{9,8},{10,9},{11,1... | collective-permute-start | bytes 9608 | tf_op jit(solution)/shard_map/ppermute | solution.py:27
  94.8 9.6 %collective-permute-start.10 = (f32[80,1,128]{2,1,0:T(1,128)S(1)}, f32[80,1,128]{2,1,0:T(1,128)S(1)}, u32[]{:S(2)}, u32[]{:S(2)}) collective-permute-start(f32[80,1,128]{2,1,0:T(1,128)S(1)} %get-tuple-element.65), channel_id=1, source_target_pairs={{0,16},{16,32},{32,48},{48,64},{64,80},{80,96},{96,112},{112,128},... | collective-permute-start | bytes 122888 | tf_op jit(solution)/shard_map/ppermute | solution.py:26
  98.6 7.4 %collective-permute-start.11 = (f32[80,1,128]{2,1,0:T(1,128)S(1)}, f32[80,1,128]{2,1,0:T(1,128)S(1)}, u32[]{:S(2)}, u32[]{:S(2)}) collective-permute-start(f32[80,1,128]{2,1,0:T(1,128)S(1)} %get-tuple-element.66), channel_id=1, source_target_pairs={{16,0},{32,16},{48,32},{64,48},{80,64},{96,80},{112,96},{128,112},... | collective-permute-start | bytes 122888 | tf_op jit(solution)/shard_map/ppermute | solution.py:27
  106.6 8.6 %collective-permute-start.12 = (f32[80,10,1]{0,2,1:T(1,128)S(1)}, f32[80,10,1]{0,2,1:T(1,128)S(1)}, u32[]{:S(2)}, u32[]{:S(2)}) collective-permute-start(f32[80,10,1]{0,2,1:T(1,128)S(1)} %copy.53), channel_id=1, source_target_pairs={{0,1},{1,2},{2,3},{3,4},{4,5},{5,6},{6,7},{7,8},{8,9},{9,10},{10,1... | collective-permute-start | bytes 9608 | tf_op jit(solution)/shard_map/ppermute | solution.py:26
  108.7 7.6 %collective-permute-start.13 = (f32[80,10,1]{0,2,1:T(1,128)S(1)}, f32[80,10,1]{0,2,1:T(1,128)S(1)}, u32[]{:S(2)}, u32[]{:S(2)}) collective-permute-start(f32[80,10,1]{0,2,1:T(1,128)S(1)} %copy.54), channel_id=1, source_target_pairs={{1,0},{2,1},{3,2},{4,3},{5,4},{6,5},{7,6},{8,7},{9,8},{10,9},{11,1... | collective-permute-start | bytes 9608 | tf_op jit(solution)/shard_map/ppermute | solution.py:27
  119.0 9.3 %collective-permute-start.14 = (f32[80,1,128]{2,1,0:T(1,128)S(1)}, f32[80,1,128]{2,1,0:T(1,128)S(1)}, u32[]{:S(2)}, u32[]{:S(2)}) collective-permute-start(f32[80,1,128]{2,1,0:T(1,128)S(1)} %get-tuple-element.63), channel_id=1, source_target_pairs={{0,16},{16,32},{32,48},{48,64},{64,80},{80,96},{96,112},{112,128},... | collective-permute-start | bytes 122888 | tf_op jit(solution)/shard_map/ppermute | solution.py:26
  125.9 7.1 %collective-permute-start.15 = (f32[80,1,128]{2,1,0:T(1,128)S(1)}, f32[80,1,128]{2,1,0:T(1,128)S(1)}, u32[]{:S(2)}, u32[]{:S(2)}) collective-permute-start(f32[80,1,128]{2,1,0:T(1,128)S(1)} %get-tuple-element.64), channel_id=1, source_target_pairs={{16,0},{32,16},{48,32},{64,48},{80,64},{96,80},{112,96},{128,112},... | collective-permute-start | bytes 122888 | tf_op jit(solution)/shard_map/ppermute | solution.py:27
  133.6 8.2 %collective-permute-start.16 = (f32[80,10,1]{0,2,1:T(1,128)S(1)}, f32[80,10,1]{0,2,1:T(1,128)S(1)}, u32[]{:S(2)}, u32[]{:S(2)}) collective-permute-start(f32[80,10,1]{0,2,1:T(1,128)S(1)} %copy.57), channel_id=1, source_target_pairs={{0,1},{1,2},{2,3},{3,4},{4,5},{5,6},{6,7},{7,8},{8,9},{9,10},{10,1... | collective-permute-start | bytes 9608 | tf_op jit(solution)/shard_map/ppermute | solution.py:26
  135.7 7.4 %collective-permute-start.17 = (f32[80,10,1]{0,2,1:T(1,128)S(1)}, f32[80,10,1]{0,2,1:T(1,128)S(1)}, u32[]{:S(2)}, u32[]{:S(2)}) collective-permute-start(f32[80,10,1]{0,2,1:T(1,128)S(1)} %copy.58), channel_id=1, source_target_pairs={{1,0},{2,1},{3,2},{4,3},{5,4},{6,5},{7,6},{8,7},{9,8},{10,9},{11,1... | collective-permute-start | bytes 9608 | tf_op jit(solution)/shard_map/ppermute | solution.py:27
where the time goes:
time: 149 us; the launch traced here: 146 us
  starting transfers between devices  95 us (64%)
  waiting for transfers between devices  25.4 us (17%)
  other arithmetic  11.8 us (8%)
  local copies, waits for them, and re-layouts  10.1 us (7%)
  matrix products  3.56 us (2%)
    ppermute x8, starting transfers between devices, padded_2(): after = lax.ppermute(first, axis, down)  46.8 us
    ppermute x8, starting transfers between devices, padded_2(): before = lax.ppermute(last, axis, up)  30.2 us
    ppermute x8, waiting for transfers between devices, padded_2(): after = lax.ppermute(first, axis, down)  10.5 us
    all_to_all x1, starting transfers between devices, on_device(): lax.all_to_all(cross_meta, 'lon', split_axis=0, concat_axis=0, tiled=True)  9.48 us
    all_to_all x1, waiting for transfers between devices, on_device(): lax.all_to_all(cross_meta, 'lon', split_axis=0, concat_axis=0, tiled=True)  8.47 us
    all_to_all x1, waiting for transfers between devices, on_device(): lax.all_to_all(crossed, 'lon', split_axis=0, concat_axis=0, tiled=True)  6.28 us
    ppermute x2, starting transfers between devices, swapped(): return lax.ppermute(value, axis, pairs)  4.33 us
    all_to_all x1, starting transfers between devices, on_device(): lax.all_to_all(crossed, 'lon', split_axis=0, concat_axis=0, tiled=True)  4.2 us
  transfers between devices with their start and end apart: 20, of which 8 were waited for; matrix products, arithmetic and copies ran while one was open for 8% of the time, Pallas kernels for 0%

commit v1 on v0

v1 whole, which is shorter than its diff:
```python
import functools

import jax
import jax.numpy as jnp
from jax import lax
from jax.experimental import pallas as pl
from jax.experimental.pallas import tpu as pltpu
from jax.sharding import PartitionSpec as P

MESH = pl.DeviceIdType.MESH
STEPS = 4
LEV = 80
ROWS = 8
LANES = 128
LINKS = 32
GROUPS = LEV // 8
EXT = ROWS + 2 * STEPS
SIDE = EXT
RATE = 0.5
F32 = jnp.float32
BF16 = jnp.bfloat16


def split3(value):
    high = value.astype(BF16)
    rest = value - high.astype(F32)
    middle = rest.astype(BF16)
    low = (rest - middle.astype(F32)).astype(BF16)
    return high, middle, low


def exact_dot(onehot, value):
    return sum(jnp.dot(onehot, part, preferred_element_type=F32) for part in split3(value))


def column(row, size):
    eye = lax.broadcasted_iota(jnp.int32, (size, size), 0) == lax.broadcasted_iota(jnp.int32, (size, size), 1)
    return jnp.sum(jnp.where(eye, jnp.broadcast_to(row, (size, size)), 0.0), axis=1, keepdims=True)


def kernel(
    n_lat,
    n_lon,
    state,
    mixing,
    diffusivity,
    weights,
    links,
    land,
    depth,
    out,
    xa,
    xb,
    surf,
    mixbuf,
    difbuf,
    wbuf,
    lkbuf,
    landbuf,
    depthbuf,
    mcat,
    pack,
    west,
    east,
    outgoing,
    incoming,
    corner_up,
    corner_down,
    from_up,
    from_down,
    flux_up,
    flux_down,
    fluxes_up,
    fluxes_down,
    load_sem,
    row_send,
    row_recv,
    side_send,
    side_recv,
    regrid_send,
    regrid_recv,
    corner_send,
    corner_recv,
    flux_send,
    flux_recv,
):
    comp, lat, lon = lax.axis_index("comp"), lax.axis_index("lat"), lax.axis_index("lon")
    other = 1 - comp
    up, down = lax.rem(lat + n_lat - 1, n_lat), lax.rem(lat + 1, n_lat)
    left, right = lax.rem(lon + n_lon - 1, n_lon), lax.rem(lon + 1, n_lon)

    barrier = pltpu.get_barrier_semaphore()
    for device in ({"lat": up}, {"lat": down}, {"lon": left}, {"lon": right}):
        pl.semaphore_signal(barrier, inc=1, device_id=device, device_id_type=MESH)
    for d in range(n_lon):
        pl.semaphore_signal(barrier, inc=1, device_id={"comp": other, "lon": d}, device_id_type=MESH)

    loads = [
        pltpu.make_async_copy(links.at[0, 0, 0], lkbuf, load_sem.at[0]),
        pltpu.make_async_copy(weights, wbuf, load_sem.at[1]),
        pltpu.make_async_copy(state.at[0, 0], surf, load_sem.at[2]),
        pltpu.make_async_copy(land, landbuf, load_sem.at[3]),
        pltpu.make_async_copy(depth, depthbuf, load_sem.at[4]),
        pltpu.make_async_copy(mixing.at[0], mixbuf, load_sem.at[5]),
        pltpu.make_async_copy(diffusivity, difbuf, load_sem.at[6]),
    ]
    for r in range(ROWS):
        loads.append(pltpu.make_async_copy(state.at[0, :, r, :], xa.at[STEPS + r], load_sem.at[7 + r]))
    for load in loads:
        load.start()

    lane = lax.broadcasted_iota(jnp.int32, (1, LANES), 1)
    cell = lane & 7
    low_half = cell < 4
    sub8 = lax.broadcasted_iota(jnp.int32, (8, LANES), 0)
    lane8 = lax.broadcasted_iota(jnp.int32, (8, LANES), 1)

    for load in loads[:3]:
        load.wait()
    table = lkbuf[...].astype(F32)
    source_row, target_row, dest_row, weight_row = (table[i : i + 1, :] for i in range(4))
    source_col, dest_col, weight_col = (column(row, LINKS) for row in (source_row, dest_row, weight_row))
    weight_ids = lax.broadcasted_iota(jnp.int32, (LINKS, wbuf.shape[1]), 1).astype(F32)
    weight = jnp.sum(
        jnp.where(weight_col == weight_ids, jnp.broadcast_to(wbuf[...], weight_ids.shape), 0.0), axis=1, keepdims=True
    )
    surface = surf[...]
    picked = jnp.zeros((LINKS, LANES), F32)
    for b in range(ROWS):
        picked = jnp.where(source_col == float(b), surface[b : b + 1, :], picked)
    row_id = lax.broadcasted_iota(jnp.int32, (n_lon * 8, LINKS), 0)
    place = (row_id.astype(F32) == target_row * 8.0 + dest_row).astype(F32).astype(BF16)
    outgoing[:, 0:8, :] = exact_dot(place, picked * weight).reshape(n_lon, 8, LANES)
    kind = row_id & 7
    dest = row_id >> 3
    before, after = dest - 1, dest + 1
    before = jnp.where(before < 0, n_lon - 1, before)
    after = jnp.where(after >= n_lon, 0, after)
    wanted = jnp.where(kind < 2, before, jnp.where((kind == 4) | (kind == 5), after, dest))
    wanted = jnp.where((kind == 3) | (kind == 7), -1, wanted)
    place_side = (wanted.astype(F32) == target_row).astype(F32).astype(BF16)
    lane32 = lax.broadcasted_iota(jnp.int32, (LINKS, LANES), 1)
    side_row = ((lane32 >> 3) - STEPS).astype(F32)
    side_weight = jnp.where(dest_col == side_row, weight, 0.0)
    ends = jnp.where(lane32 < 8, pltpu.roll(picked, 4, 1), 0.0)
    for shift in (8, 16, 32, 64):
        ends = ends + pltpu.roll(ends, shift, 1)
    both = exact_dot(place_side, jnp.concatenate([side_weight * ends, side_weight], axis=1))
    both = both.reshape(n_lon, 8, 2 * LANES)
    kind3 = lax.broadcasted_iota(jnp.int32, (n_lon, 8, LANES), 1)
    merged = jnp.where((kind3 & 3) == 0, both[:, :, :LANES], both[:, :, LANES:])
    outgoing[:, 8:16, :] = jnp.where(low_half, merged, pltpu.roll(merged, 4, 1))

    loads[3].wait()
    loads[4].wait()
    land_col = landbuf[...].astype(F32)
    depth_col = jnp.where(comp == 1, land_col * depthbuf[...].astype(F32), float(LEV))
    land_own = jnp.broadcast_to(land_col, (8, LANES))
    depth_own = jnp.broadcast_to(depth_col, (8, LANES))
    mine = (lane8 >> 3) == sub8
    depth_ends = jnp.sum(jnp.where(mine, depth_own, 0.0), axis=0, keepdims=True)
    land_ends = jnp.sum(jnp.where(mine, land_own, 0.0), axis=0, keepdims=True)
    pack[5 * 8 :, :] = jnp.where(sub8 == 0, depth_ends, land_ends)

    for load in loads[7:]:
        load.wait()

    def gather_ends(src, rows, offset):
        total = None
        for e in rows:
            rolled = pltpu.roll(src[e], (e * 8 + 4) % LANES, 1)
            total = rolled if total is None else jnp.where((lane >> 3) == e, rolled, total)
        return total

    own_ends = gather_ends(xa, range(STEPS, STEPS + ROWS), 0)
    lower = pltpu.roll(own_ends[: LEV // 2], LANES - 32, 1)
    upper = pltpu.roll(own_ends[LEV // 2 :], 32, 1)
    pack[: LEV // 2, :] = jnp.where(lane < 64, lower, upper)

    pl.semaphore_wait(barrier, 4 + n_lon)

    to_right = pltpu.make_async_remote_copy(
        pack, west, side_send.at[0], side_recv.at[0], device_id={"lon": right}, device_id_type=MESH
    )
    to_left = pltpu.make_async_remote_copy(
        pack, east, side_send.at[1], side_recv.at[1], device_id={"lon": left}, device_id_type=MESH
    )
    to_right.start()
    to_left.start()
    regrids = []
    for k in sorted(range(n_lon), key=lambda k: -min(k % 8, 8 - k % 8)):
        d = lax.rem(lon + k, n_lon)
        copy = pltpu.make_async_remote_copy(
            outgoing.at[d, 0:11],
            incoming.at[lon, 0:11],
            regrid_send.at[k],
            regrid_recv.at[lon],
            device_id={"comp": other, "lon": d},
            device_id_type=MESH,
        )
        copy.start()
        regrids.append(copy)
    rows_out = []
    for ring in range(STEPS):
        rows_out.append(
            pltpu.make_async_remote_copy(
                xa.at[STEPS + ring],
                xa.at[STEPS + ROWS + ring],
                row_send.at[2 * ring],
                row_recv.at[2 * ring],
                device_id={"lat": up},
                device_id_type=MESH,
            )
        )
        rows_out.append(
            pltpu.make_async_remote_copy(
                xa.at[STEPS + ROWS - 1 - ring],
                xa.at[STEPS - 1 - ring],
                row_send.at[2 * ring + 1],
                row_recv.at[2 * ring + 1],
                device_id={"lat": down},
                device_id_type=MESH,
            )
        )
    for copy in rows_out[:4]:
        copy.start()

    loads[5].wait()
    loads[6].wait()
    mix = mixbuf[...]
    mix_high = mix.astype(BF16).astype(F32)
    mcat[:, 0:LEV] = mix_high
    mcat[:, LEV : 2 * LEV] = mix_high
    mcat[:, 2 * LEV : 3 * LEV] = mix - mix_high
    mcat[:, 3 * LEV :] = jnp.zeros((LEV, 16), F32)
    operator = mcat[...].astype(BF16)
    diffuse = jnp.broadcast_to(column(difbuf[...], LEV), (LEV, LANES))
    level = lax.broadcasted_iota(jnp.int32, (LEV, LANES), 0).astype(F32)

    to_right.wait_recv()
    to_left.wait_recv()
    arrived = jnp.where(low_half, west[...], east[...])
    side_own = jnp.concatenate(
        [pltpu.roll(arrived[: LEV // 2], 32, 1), pltpu.roll(arrived[: LEV // 2], LANES - 32, 1)], axis=0
    )
    masks = pltpu.roll(arrived[LEV // 2 :], 32, 1)
    depth_side, land_side = masks[0:1], masks[1:2]

    def corner(target, base):
        for v in range(3):
            groups = range(v * 4, min(v * 4 + 4, GROUPS))
            total = None
            for m, g in enumerate(groups):
                rolled = pltpu.roll(side_own[g * 8 : g * 8 + 8], (m * 32 - base) % LANES, 1)
                total = rolled if total is None else jnp.where((lane >> 5) == m, rolled, total)
            if v == 2:
                total = jnp.where((lane >> 5) == 2, pltpu.roll(jnp.broadcast_to(depth_side, (8, LANES)), (64 - base) % LANES, 1), total)
            target[v * 8 : v * 8 + 8, :] = total
        target[24:32, :] = depth_own

    corner(corner_up, 32)
    corner(corner_down, 64)
    corner_to_up = pltpu.make_async_remote_copy(
        corner_up, from_down, corner_send.at[0], corner_recv.at[0], device_id={"lat": up}, device_id_type=MESH
    )
    corner_to_down = pltpu.make_async_remote_copy(
        corner_down, from_up, corner_send.at[1], corner_recv.at[1], device_id={"lat": down}, device_id_type=MESH
    )
    corner_to_up.start()
    corner_to_down.start()
    for copy in rows_out[4:]:
        copy.start()

    for j in range(n_lon):
        pltpu.make_async_remote_copy(
            outgoing.at[j, 0:11],
            incoming.at[j, 0:11],
            regrid_send.at[j],
            regrid_recv.at[j],
            device_id={"comp": other, "lon": j},
            device_id_type=MESH,
        ).wait_recv()
    accum = incoming[0, 0:8, :]
    extra = incoming[0, 8:11, :]
    for j in range(1, n_lon):
        accum = accum + incoming[j, 0:8, :]
        extra = extra + incoming[j, 8:11, :]
    totals = jnp.sum(
        jnp.where(lane8 == (sub8 + STEPS) * 8, jnp.broadcast_to(extra[2:3], (8, LANES)), 0.0), axis=1, keepdims=True
    )
    flux_own = RATE * land_own * (accum / jnp.maximum(totals, 1.0) - surface)
    flux_side = RATE * land_side * (extra[0:1] / jnp.maximum(extra[1:2], 1.0) - side_own[0:1])
    flux_up[...] = jnp.where(sub8 < 3, flux_own, flux_side)
    flux_down[...] = jnp.where(sub8 >= 5, flux_own, flux_side)
    flux_to_up = pltpu.make_async_remote_copy(
        flux_up, fluxes_down, flux_send.at[0], flux_recv.at[0], device_id={"lat": up}, device_id_type=MESH
    )
    flux_to_down = pltpu.make_async_remote_copy(
        flux_down, fluxes_up, flux_send.at[1], flux_recv.at[1], device_id={"lat": down}, device_id_type=MESH
    )
    flux_to_up.start()
    flux_to_down.start()

    keep_up = jnp.where(lat > 0, 1.0, 0.0)
    keep_down = jnp.where(lat < n_lat - 1, 1.0, 0.0)
    corner_to_up.wait_recv()
    corner_to_down.wait_recv()
    above, below = from_up[...], from_down[...]
    sides = []
    for g in range(GROUPS):
        v, m = divmod(g, 4)
        top = pltpu.roll(above[v * 8 : v * 8 + 8], (0 - m * 32) % LANES, 1) * keep_up
        bottom = pltpu.roll(below[v * 8 : v * 8 + 8], (96 - m * 32) % LANES, 1) * keep_down
        sides.append(jnp.where(lane < 32, top, jnp.where(lane >= 96, bottom, side_own[g * 8 : g * 8 + 8])))
    xa[SIDE] = jnp.concatenate(sides, axis=0)
    depth_top = pltpu.roll(above[16:17], LANES - 64, 1) * keep_up
    depth_bottom = pltpu.roll(below[16:17], 32, 1) * keep_down
    depth_z = jnp.where(lane < 32, depth_top, jnp.where(lane >= 96, depth_bottom, depth_side))
    depths = (
        [above[28 + e : 29 + e] * keep_up for e in range(4)]
        + [depth_own[r : r + 1] for r in range(ROWS)]
        + [below[24 + e : 25 + e] * keep_down for e in range(4)]
        + [depth_z]
    )
    flux_to_up.wait_recv()
    flux_to_down.wait_recv()
    top_flux, bottom_flux = fluxes_up[...], fluxes_down[...]
    flux_z = jnp.where(
        lane < 32,
        pltpu.roll(top_flux[0:1], 64, 1),
        jnp.where(lane >= 96, pltpu.roll(bottom_flux[3:4], 64, 1), flux_side),
    )
    fluxes = (
        [None]
        + [top_flux[5 + e : 6 + e] for e in range(3)]
        + [flux_own[r : r + 1] for r in range(ROWS)]
        + [bottom_flux[e : e + 1] for e in range(3)]
        + [None, flux_z]
    )
    for copy in rows_out:
        copy.wait()

    @pl.when(lat == 0)
    def _():
        xa[0:STEPS] = jnp.zeros((STEPS, LEV, LANES), F32)

    @pl.when(lat == n_lat - 1)
    def _():
        xa[STEPS + ROWS : EXT] = jnp.zeros((STEPS, LEV, LANES), F32)

    first_lane, last_lane = lane == 0, lane == LANES - 1
    pad = jnp.zeros((16, LANES), BF16)

    def operand(centre, neighbours, e):
        moved = centre + diffuse * (neighbours - 4.0 * centre)
        moved = jnp.concatenate([moved[:8] + jnp.where(sub8 == 0, fluxes[e], 0.0), moved[8:]], axis=0)
        active = level < depths[e]
        moved = jnp.where(active, moved, 0.0)
        high = moved.astype(BF16)
        low = (moved - high.astype(F32)).astype(BF16)
        return active, jnp.concatenate([high, low, high, pad], axis=0)

    def side_operand(src, rows):
        z = src[SIDE]
        ends = gather_ends(src, rows, 0)
        from_west = pltpu.roll(jnp.where(cell == 3, ends, z), 1, 1)
        from_east = pltpu.roll(jnp.where(cell == 4, ends, z), LANES - 1, 1)
        neighbours = pltpu.roll(z, 8, 1) + pltpu.roll(z, LANES - 8, 1) + from_west + from_east
        return operand(z, neighbours, SIDE)

    def row_operand(src, e):
        centre = src[e]
        z = pltpu.roll(src[SIDE], (LANES - (e * 8 + 4)) % LANES, 1)
        from_west = pltpu.roll(jnp.where(last_lane, z, centre), 1, 1)
        from_east = pltpu.roll(jnp.where(first_lane, z, centre), LANES - 1, 1)
        return operand(centre, src[e - 1] + src[e + 1] + from_west + from_east, e)

    stores = []
    for step in range(1, STEPS + 1):
        src, dst = (xa, xb) if step % 2 else (xb, xa)
        rows = list(range(step, EXT - step))
        tiles = rows + ([SIDE] if step < STEPS else [])
        for at in range(0, len(tiles), 2):
            pair = tiles[at : at + 2]
            parts = [side_operand(src, rows) if e == SIDE else row_operand(src, e) for e in pair]
            right_side = parts[0][1] if len(pair) == 1 else jnp.concatenate([p[1] for p in parts], axis=1)
            mixed = jnp.dot(operator, right_side, preferred_element_type=F32)
            for i, e in enumerate(pair):
                dst[e] = jnp.where(parts[i][0], mixed[:, i * LANES : (i + 1) * LANES], src[e])
                if step == STEPS:
                    store = pltpu.make_async_copy(
                        dst.at[e], out.at[0, :, e - STEPS, :], load_sem.at[7 + e - STEPS]
                    )
                    store.start()
                    stores.append(store)
    for copy in (to_right, to_left, corner_to_up, corner_to_down, flux_to_up, flux_to_down, *regrids):
        copy.wait_send()
    for store in stores:
        store.wait()


def on_device(n_lat, n_lon, state, mixing, diffusivity, weights, links, land, depth):
    vmem = pltpu.VMEM
    dma = pltpu.SemaphoreType.DMA
    return pl.pallas_call(
        functools.partial(kernel, n_lat, n_lon),
        out_shape=jax.ShapeDtypeStruct(state.shape, F32),
        in_specs=[pl.BlockSpec(memory_space=pl.ANY)] * 7,
        out_specs=pl.BlockSpec(memory_space=pl.ANY),
        scratch_shapes=[
            vmem((EXT + 1, LEV, LANES), F32),
            vmem((EXT + 1, LEV, LANES), F32),
            vmem((8, LANES), F32),
            vmem((LEV, LEV), F32),
            vmem(diffusivity.shape, F32),
            vmem(weights.shape, F32),
            vmem((4, LINKS), jnp.int32),
            vmem(land.shape, jnp.int32),
            vmem(depth.shape, jnp.int32),
            vmem((LEV, 3 * LEV + 16), F32),
            vmem((LEV // 2 + 8, LANES), F32),
            vmem((LEV // 2 + 8, LANES), F32),
            vmem((LEV // 2 + 8, LANES), F32),
            vmem((n_lon, 16, LANES), F32),
            vmem((n_lon, 16, LANES), F32),
            vmem((32, LANES), F32),
            vmem((32, LANES), F32),
            vmem((32, LANES), F32),
            vmem((32, LANES), F32),
            vmem((8, LANES), F32),
            vmem((8, LANES), F32),
            vmem((8, LANES), F32),
            vmem((8, LANES), F32),
            dma((7 + ROWS,)),
            dma((2 * STEPS,)),
            dma((2 * STEPS,)),
            dma((2,)),
            dma((2,)),
            dma((n_lon,)),
            dma((n_lon,)),
            dma((2,)),
            dma((2,)),
            dma((2,)),
            dma((2,)),
        ],
        compiler_params=pltpu.CompilerParams(collective_id=0, has_side_effects=True),
    )(state, mixing, diffusivity, weights, links, land, depth)


def solution(mesh):
    in_specs = (
        P("comp", None, "lat", "lon"),
        P("comp", None, None),
        P("comp", None),
        P("comp", None),
        P("comp", "lat", "lon", None, None),
        P("lat", "lon"),
        P("lat", "lon"),
    )
    return jax.shard_map(
        functools.partial(on_device, mesh.shape["lat"], mesh.shape["lon"]),
        mesh=mesh,
        in_specs=in_specs,
        out_specs=P("comp", None, "lat", "lon"),
        check_vma=False,
    )
```

time: 149 us -> 44.3 us (0.30)
  the two profiles are of different devices: /device:TPU:14 before, /device:TPU:1 now
where the time goes in v1:
time: 44.3 us; the launch traced here: 44 us
  Pallas kernels  40.3 us (91%)
  local copies, waits for them, and re-layouts  3.73 us (8%)
    pallas_call x1, Pallas kernels, on_device(): pl.pallas_call(functools.partial(kernel, n_lat, n_lon), out_shape=jax.Sha...  40.3 us
    unnamed x5, local copies, waits for them, and re-layouts  3.73 us

profile of v1, /device:TPU:1, one launch (start us, length us, event | category | flops | bytes accessed | tf_op | source)
XLA Modules:
  0.0 44.0 jit_solution(5319723257059860866)
XLA Ops:
  0.0 0.0 copy-start
  0.0 1.3 %copy.8.land = s32[8,1]{1,0:T(8,128)} copy(s32[8,1]{0,1:T(1,128)} %param.12) | data formatting | bytes 64 | tf_op args[5]
  1.3 0.0 copy-done
  1.3 0.7 %copy.9.depth = s32[8,1]{1,0:T(8,128)} copy(s32[8,1]{0,1:T(1,128)S(1)} %copy-done) | data formatting | bytes 64 | tf_op args[6]
  2.0 40.3 %shard_map.73 = f32[1,80,8,128]{3,2,1,0:T(8,128)} custom-call(f32[1,80,8,128]{3,2,1,0:T(8,128)} %state.1, f32[1,80,80]{2,1,0:T(8,128)} %mixing.1, f32[1,80]{1,0:T(1,128)} %diffusivity.1, f32[1,64]{1,0:T(1,128)} %weights.1, s32[1,1,1,4,32]{4,3,2,1,0:T(4,128)} %links.1, s32[8,1]{1,0:T(8,128)} %copy.8.land, s32[8,1]{1,0:T(8,128)} %copy.9.depth), custom_call_target="tpu_custom_call" | custom-call | tf_op jit(solution)/shard_map/pallas_call | solution.py:405
  42.3 1.7 %copy.11 = f32[1,80,8,128]{3,2,1,0:T(8,128)} copy(f32[1,80,8,128]{3,2,1,0:T(8,128)} %shard_map.73) | data formatting | bytes 655360
Async XLA Ops:
  0.0 1.3 %copy-start = (s32[8,1]{0,1:T(1,128)S(1)}, s32[8,1]{0,1:T(1,128)}, u32[]{:S(2)}) copy-start(s32[8,1]{0,1:T(1,128)} %param.13) | copy-start | bytes 100

commit v2 on v1

--- a/solution.py
+++ b/solution.py
@@ -29,7 +29,7 @@
     return high, middle, low
 
 
-def exact_dot(onehot, value):
+def ex0ct_dot(onehot, value):
     return sum(jnp.dot(onehot, part, preferred_element_type=F32) for part in split3(value))
 
 
@@ -49,8 +49,11 @@
     land,
     depth,
     out,
-    xa,
-    xb,
+    x0,
+    x1,
+    x2,
+    x3,
+    x4,
     surf,
     mixbuf,
     difbuf,
@@ -83,17 +86,42 @@
     corner_recv,
     flux_send,
     flux_recv,
+    handing,
+    given,
+    hand_send,
+    hand_recv,
 ):
     comp, lat, lon = lax.axis_index("comp"), lax.axis_index("lat"), lax.axis_index("lon")
     other = 1 - comp
     up, down = lax.rem(lat + n_lat - 1, n_lat), lax.rem(lat + 1, n_lat)
     left, right = lax.rem(lon + n_lon - 1, n_lon), lax.rem(lon + 1, n_lon)
 
+    has_up, has_down = lat > 0, lat < n_lat - 1
     barrier = pltpu.get_barrier_semaphore()
-    for device in ({"lat": up}, {"lat": down}, {"lon": left}, {"lon": right}):
+
+    def greet(device):
         pl.semaphore_signal(barrier, inc=1, device_id=device, device_id_type=MESH)
-    for d in range(n_lon):
-        pl.semaphore_signal(barrier, inc=1, device_id={"comp": other, "lon": d}, device_id_type=MESH)
+
+    @pl.when(comp == 1)
+    def _():
+        for k in range(n_lon):
+            greet({"comp": 0, "lon": lax.rem(lon + k, n_lon)})
+        for k in range(1, n_lon):
+            greet({"lon": lax.rem(lon + k, n_lon)})
+
+    @pl.when(comp == 0)
+    def _():
+        greet({"comp": 1})
+        greet({"lon": left})
+        greet({"lon": right})
+
+    @pl.when(has_up)
+    def _():
+        greet({"lat": up})
+
+    @pl.when(has_down)
+    def _():
+        greet({"lat": down})
 
     loads = [
         pltpu.make_async_copy(links.at[0, 0, 0], lkbuf, load_sem.at[0]),
@@ -105,9 +133,21 @@
         pltpu.make_async_copy(diffusivity, difbuf, load_sem.at[6]),
     ]
     for r in range(ROWS):
-        loads.append(pltpu.make_async_copy(state.at[0, :, r, :], xa.at[STEPS + r], load_sem.at[7 + r]))
+        loads.append(pltpu.make_async_copy(state.at[0, :, r, :], x0.at[STEPS + r], load_sem.at[7 + r]))
     for load in loads:
         load.start()
+
+    @pl.when(lat == 0)
+    def _():
+        x0[0:STEPS] = jnp.zeros((STEPS, LEV, LANES), F32)
+        from_up[...] = jnp.zeros((32, LANES), F32)
+        fluxes_up[...] = jnp.zeros((8, LANES), F32)
+
+    @pl.when(lat == n_lat - 1)
+    def _():
+        x0[STEPS + ROWS : EXT] = jnp.zeros((STEPS, LEV, LANES), F32)
+        from_down[...] = jnp.zeros((32, LANES), F32)
+        fluxes_down[...] = jnp.zeros((8, LANES), F32)
 
     lane = lax.broadcasted_iota(jnp.int32, (1, LANES), 1)
     cell = lane & 7
@@ -130,7 +170,7 @@
         picked = jnp.where(source_col == float(b), surface[b : b + 1, :], picked)
     row_id = lax.broadcasted_iota(jnp.int32, (n_lon * 8, LINKS), 0)
     place = (row_id.astype(F32) == target_row * 8.0 + dest_row).astype(F32).astype(BF16)
-    outgoing[:, 0:8, :] = exact_dot(place, picked * weight).reshape(n_lon, 8, LANES)
+    outgoing[:, 0:8, :] = ex0ct_dot(place, picked * weight).reshape(n_lon, 8, LANES)
     kind = row_id & 7
     dest = row_id >> 3
     before, after = dest - 1, dest + 1
@@ -145,7 +185,7 @@
     ends = jnp.where(lane32 < 8, pltpu.roll(picked, 4, 1), 0.0)
     for shift in (8, 16, 32, 64):
         ends = ends + pltpu.roll(ends, shift, 1)
-    both = exact_dot(place_side, jnp.concatenate([side_weight * ends, side_weight], axis=1))
+    both = ex0ct_dot(place_side, jnp.concatenate([side_weight * ends, side_weight], axis=1))
     both = both.reshape(n_lon, 8, 2 * LANES)
     kind3 = lax.broadcasted_iota(jnp.int32, (n_lon, 8, LANES), 1)
     merged = jnp.where((kind3 & 3) == 0, both[:, :, :LANES], both[:, :, LANES:])
@@ -153,8 +193,9 @@
 
     loads[3].wait()
     loads[4].wait()
-    land_col = landbuf[...].astype(F32)
-    depth_col = jnp.where(comp == 1, land_col * depthbuf[...].astype(F32), float(LEV))
+    land_row = landbuf[...].astype(F32)
+    depth_row = jnp.where(comp == 1, land_row * depthbuf[...].astype(F32), float(LEV))
+    land_col, depth_col = column(land_row, ROWS), column(depth_row, ROWS)
     land_own = jnp.broadcast_to(land_col, (8, LANES))
     depth_own = jnp.broadcast_to(depth_col, (8, LANES))
     mine = (lane8 >> 3) == sub8
@@ -172,12 +213,14 @@
             total = rolled if total is None else jnp.where((lane >> 3) == e, rolled, total)
         return total
 
-    own_ends = gather_ends(xa, range(STEPS, STEPS + ROWS), 0)
+    own_ends = gather_ends(x0, range(STEPS, STEPS + ROWS), 0)
     lower = pltpu.roll(own_ends[: LEV // 2], LANES - 32, 1)
     upper = pltpu.roll(own_ends[LEV // 2 :], 32, 1)
     pack[: LEV // 2, :] = jnp.where(lane < 64, lower, upper)
 
-    pl.semaphore_wait(barrier, 4 + n_lon)
+    above_here = 1 - lax.div(n_lat - lat, n_lat)
+    below_here = 1 - lax.div(lat + 1, n_lat)
+    pl.semaphore_wait(barrier, n_lon + 2 * (1 - comp) + above_here + below_here)
 
     to_right = pltpu.make_async_remote_copy(
         pack, west, side_send.at[0], side_recv.at[0], device_id={"lon": right}, device_id_type=MESH
@@ -187,25 +230,37 @@
     )
     to_right.start()
     to_left.start()
-    regrids = []
-    for k in sorted(range(n_lon), key=lambda k: -min(k % 8, 8 - k % 8)):
+
+    def regrid(k):
         d = lax.rem(lon + k, n_lon)
-        copy = pltpu.make_async_remote_copy(
+        return pltpu.make_async_remote_copy(
             outgoing.at[d, 0:11],
-            incoming.at[lon, 0:11],
+            incoming.at[comp, lon, 0:11],
             regrid_send.at[k],
-            regrid_recv.at[lon],
-            device_id={"comp": other, "lon": d},
+            regrid_recv.at[comp, lon],
+            device_id={"comp": 1, "lon": d},
             device_id_type=MESH,
         )
-        copy.start()
-        regrids.append(copy)
+
+    for k in sorted(range(1, n_lon), key=lambda k: -min(k % 8, 8 - k % 8)):
+        regrid(k).start()
+
+    @pl.when(comp == 0)
+    def _():
+        regrid(0).start()
+
+    kept = pltpu.make_async_copy(outgoing.at[lon, 0:11], incoming.at[1, lon, 0:11], regrid_recv.at[1, lon])
+
+    @pl.when(comp == 1)
+    def _():
+        kept.start()
+
     rows_out = []
     for ring in range(STEPS):
         rows_out.append(
             pltpu.make_async_remote_copy(
-                xa.at[STEPS + ring],
-                xa.at[STEPS + ROWS + ring],
+                x0.at[STEPS + ring],
+                x0.at[STEPS + ROWS + ring],
                 row_send.at[2 * ring],
                 row_recv.at[2 * ring],
                 device_id={"lat": up},
@@ -214,16 +269,30 @@
         )
         rows_out.append(
             pltpu.make_async_remote_copy(
-                xa.at[STEPS + ROWS - 1 - ring],
-                xa.at[STEPS - 1 - ring],
+                x0.at[STEPS + ROWS - 1 - ring],
+                x0.at[STEPS - 1 - ring],
                 row_send.at[2 * ring + 1],
                 row_recv.at[2 * ring + 1],
                 device_id={"lat": down},
                 device_id_type=MESH,
             )
         )
-    for copy in rows_out[:4]:
-        copy.start()
+
+    def both_ways(act, upward, downward):
+        @pl.when(has_up)
+        def _():
+            for copy in upward:
+                act(copy)
+
+        @pl.when(has_down)
+        def _():
+            for copy in downward:
+                act(copy)
+
+    start = lambda copy: copy.start()
+    arrive = lambda copy: copy.wait_recv()
+    leave = lambda copy: copy.wait_send()
+    both_ways(start, rows_out[0:4:2], rows_out[1:4:2])
 
     loads[5].wait()
     loads[6].wait()
@@ -266,25 +335,44 @@
     corner_to_down = pltpu.make_async_remote_copy(
         corner_down, from_up, corner_send.at[1], corner_recv.at[1], device_id={"lat": down}, device_id_type=MESH
     )
-    corner_to_up.start()
-    corner_to_down.start()
-    for copy in rows_out[4:]:
-        copy.start()
-
-    for j in range(n_lon):
-        pltpu.make_async_remote_copy(
-            outgoing.at[j, 0:11],
-            incoming.at[j, 0:11],
-            regrid_send.at[j],
-            regrid_recv.at[j],
-            device_id={"comp": other, "lon": j},
-            device_id_type=MESH,
-        ).wait_recv()
-    accum = incoming[0, 0:8, :]
-    extra = incoming[0, 8:11, :]
-    for j in range(1, n_lon):
-        accum = accum + incoming[j, 0:8, :]
-        extra = extra + incoming[j, 8:11, :]
+    both_ways(start, [corner_to_up, *rows_out[4::2]], [corner_to_down, *rows_out[5::2]])
+
+    handed = pltpu.make_async_remote_copy(
+        handing, given, hand_send, hand_recv, device_id={"comp": 0}, device_id_type=MESH
+    )
+
+    def gathered(section):
+        for j in range(n_lon):
+            copy = pltpu.make_async_remote_copy(
+                outgoing.at[j, 0:11],
+                incoming.at[section, j, 0:11],
+                regrid_send.at[j],
+                regrid_recv.at[section, j],
+                device_id={"comp": 1, "lon": j},
+                device_id_type=MESH,
+            )
+            copy.wait_recv()
+        accum, extra = incoming[section, 0, 0:8, :], incoming[section, 0, 8:11, :]
+        for j in range(1, n_lon):
+            accum = accum + incoming[section, j, 0:8, :]
+            extra = extra + incoming[section, j, 8:11, :]
+        return accum, extra
+
+    @pl.when(comp == 1)
+    def _():
+        accum, extra = gathered(1)
+        handing[0:8, :] = accum
+        handing[8:11, :] = extra
+        handed.start()
+        accum, extra = gathered(0)
+        given[0:8, :] = accum
+        given[8:11, :] = extra
+
+    @pl.when(comp == 0)
+    def _():
+        handed.wait_recv()
+
+    accum, extra = given[0:8, :], given[8:11, :]
     totals = jnp.sum(
         jnp.where(lane8 == (sub8 + STEPS) * 8, jnp.broadcast_to(extra[2:3], (8, LANES)), 0.0), axis=1, keepdims=True
     )
@@ -298,60 +386,15 @@
     flux_to_down = pltpu.make_async_remote_copy(
         flux_down, fluxes_up, flux_send.at[1], flux_recv.at[1], device_id={"lat": down}, device_id_type=MESH
     )
-    flux_to_up.start()
-    flux_to_down.start()
-
-    keep_up = jnp.where(lat > 0, 1.0, 0.0)
-    keep_down = jnp.where(lat < n_lat - 1, 1.0, 0.0)
-    corner_to_up.wait_recv()
-    corner_to_down.wait_recv()
-    above, below = from_up[...], from_down[...]
-    sides = []
-    for g in range(GROUPS):
-        v, m = divmod(g, 4)
-        top = pltpu.roll(above[v * 8 : v * 8 + 8], (0 - m * 32) % LANES, 1) * keep_up
-        bottom = pltpu.roll(below[v * 8 : v * 8 + 8], (96 - m * 32) % LANES, 1) * keep_down
-        sides.append(jnp.where(lane < 32, top, jnp.where(lane >= 96, bottom, side_own[g * 8 : g * 8 + 8])))
-    xa[SIDE] = jnp.concatenate(sides, axis=0)
-    depth_top = pltpu.roll(above[16:17], LANES - 64, 1) * keep_up
-    depth_bottom = pltpu.roll(below[16:17], 32, 1) * keep_down
-    depth_z = jnp.where(lane < 32, depth_top, jnp.where(lane >= 96, depth_bottom, depth_side))
-    depths = (
-        [above[28 + e : 29 + e] * keep_up for e in range(4)]
-        + [depth_own[r : r + 1] for r in range(ROWS)]
-        + [below[24 + e : 25 + e] * keep_down for e in range(4)]
-        + [depth_z]
-    )
-    flux_to_up.wait_recv()
-    flux_to_down.wait_recv()
-    top_flux, bottom_flux = fluxes_up[...], fluxes_down[...]
-    flux_z = jnp.where(
-        lane < 32,
-        pltpu.roll(top_flux[0:1], 64, 1),
-        jnp.where(lane >= 96, pltpu.roll(bottom_flux[3:4], 64, 1), flux_side),
-    )
-    fluxes = (
-        [None]
-        + [top_flux[5 + e : 6 + e] for e in range(3)]
-        + [flux_own[r : r + 1] for r in range(ROWS)]
-        + [bottom_flux[e : e + 1] for e in range(3)]
-        + [None, flux_z]
-    )
-    for copy in rows_out:
-        copy.wait()
-
-    @pl.when(lat == 0)
-    def _():
-        xa[0:STEPS] = jnp.zeros((STEPS, LEV, LANES), F32)
-
-    @pl.when(lat == n_lat - 1)
-    def _():
-        xa[STEPS + ROWS : EXT] = jnp.zeros((STEPS, LEV, LANES), F32)
+    both_ways(start, [flux_to_up], [flux_to_down])
 
     first_lane, last_lane = lane == 0, lane == LANES - 1
     pad = jnp.zeros((16, LANES), BF16)
-
-    def operand(centre, neighbours, e):
+    levels_at = (x0, x1, x2, x3, x4)
+    depths = {STEPS + r: depth_own[r : r + 1] for r in range(ROWS)}
+    fluxes = {STEPS + r: flux_own[r : r + 1] for r in range(ROWS)}
+
+    def operand(centre, neighbours, e, step):
         moved = centre + diffuse * (neighbours - 4.0 * centre)
         moved = jnp.concatenate([moved[:8] + jnp.where(sub8 == 0, fluxes[e], 0.0), moved[8:]], axis=0)
         active = level < depths[e]
@@ -360,41 +403,97 @@
         low = (moved - high.astype(F32)).astype(BF16)
         return active, jnp.concatenate([high, low, high, pad], axis=0)
 
-    def side_operand(src, rows):
+    def side_operand(src, rows, step):
         z = src[SIDE]
         ends = gather_ends(src, rows, 0)
         from_west = pltpu.roll(jnp.where(cell == 3, ends, z), 1, 1)
         from_east = pltpu.roll(jnp.where(cell == 4, ends, z), LANES - 1, 1)
         neighbours = pltpu.roll(z, 8, 1) + pltpu.roll(z, LANES - 8, 1) + from_west + from_east
-        return operand(z, neighbours, SIDE)
-
-    def row_operand(src, e):
+        return operand(z, neighbours, SIDE, step)
+
+    def row_operand(src, e, step):
         centre = src[e]
         z = pltpu.roll(src[SIDE], (LANES - (e * 8 + 4)) % LANES, 1)
         from_west = pltpu.roll(jnp.where(last_lane, z, centre), 1, 1)
         from_east = pltpu.roll(jnp.where(first_lane, z, centre), LANES - 1, 1)
-        return operand(centre, src[e - 1] + src[e + 1] + from_west + from_east, e)
+        return operand(centre, src[e - 1] + src[e + 1] + from_west + from_east, e, step)
 
     stores = []
-    for step in range(1, STEPS + 1):
-        src, dst = (xa, xb) if step % 2 else (xb, xa)
-        rows = list(range(step, EXT - step))
+
+    def advance(step, rows, merge):
+        src, dst = levels_at[step - 1], levels_at[step]
         tiles = rows + ([SIDE] if step < STEPS else [])
         for at in range(0, len(tiles), 2):
             pair = tiles[at : at + 2]
-            parts = [side_operand(src, rows) if e == SIDE else row_operand(src, e) for e in pair]
+            parts = [side_operand(src, rows, step) if e == SIDE else row_operand(src, e, step) for e in pair]
             right_side = parts[0][1] if len(pair) == 1 else jnp.concatenate([p[1] for p in parts], axis=1)
             mixed = jnp.dot(operator, right_side, preferred_element_type=F32)
             for i, e in enumerate(pair):
-                dst[e] = jnp.where(parts[i][0], mixed[:, i * LANES : (i + 1) * LANES], src[e])
+                new = jnp.where(parts[i][0], mixed[:, i * LANES : (i + 1) * LANES], src[e])
+                if e == SIDE and merge:
+                    new = jnp.where((lane >> 3) <= rows[-1], new, dst[e])
                 if step == STEPS:
-                    store = pltpu.make_async_copy(
-                        dst.at[e], out.at[0, :, e - STEPS, :], load_sem.at[7 + e - STEPS]
-                    )
+                    r = e - STEPS
+                    dst[r] = new
+                    store = pltpu.make_async_copy(dst.at[r], out.at[0, :, r, :], load_sem.at[7 + r])
                     store.start()
                     stores.append(store)
-    for copy in (to_right, to_left, corner_to_up, corner_to_down, flux_to_up, flux_to_down, *regrids):
+                else:
+                    dst[e] = new
+
+    both_ways(arrive, [], [corner_to_up])
+    below = from_down[...]
+    sides = []
+    for g in range(GROUPS):
+        v, m = divmod(g, 4)
+        bottom = pltpu.roll(below[v * 8 : v * 8 + 8], (96 - m * 32) % LANES, 1)
+        sides.append(jnp.where(lane >= 96, bottom, side_own[g * 8 : g * 8 + 8]))
+    x0[SIDE] = jnp.concatenate(sides, axis=0)
+    depth_part = jnp.where(lane >= 96, pltpu.roll(below[16:17], 32, 1), depth_side)
+    depths.update({STEPS + ROWS + e: below[24 + e : 25 + e] for e in range(4)})
+    depths[SIDE] = depth_part
+    both_ways(arrive, [], [flux_to_up])
+    bottom_flux = fluxes_down[...]
+    flux_part = jnp.where(lane >= 96, pltpu.roll(bottom_flux[3:4], 64, 1), flux_side)
+    fluxes.update({STEPS + ROWS + e: bottom_flux[e : e + 1] for e in range(3)})
+    fluxes[SIDE] = flux_part
+    both_ways(arrive, [], rows_out[0::2])
+    for step in range(1, STEPS + 1):
+        advance(step, list(range(STEPS + step, EXT - step)), False)
+
+    both_ways(arrive, [corner_to_down], [])
+    above = from_up[...]
+    sides = []
+    for g in range(GROUPS):
+        v, m = divmod(g, 4)
+        top = pltpu.roll(above[v * 8 : v * 8 + 8], (0 - m * 32) % LANES, 1)
+        sides.append(jnp.where(lane < 32, top, x0[SIDE, g * 8 : g * 8 + 8]))
+    x0[SIDE] = jnp.concatenate(sides, axis=0)
+    depths[SIDE] = jnp.where(lane < 32, pltpu.roll(above[16:17], LANES - 64, 1), depth_part)
+    depths.update({e: above[28 + e : 29 + e] for e in range(4)})
+    both_ways(arrive, [flux_to_down], [])
+    top_flux = fluxes_up[...]
+    fluxes[SIDE] = jnp.where(lane < 32, pltpu.roll(top_flux[0:1], 64, 1), flux_part)
+    fluxes.update({1 + e: top_flux[5 + e : 6 + e] for e in range(3)})
+    both_ways(arrive, rows_out[1:4:2], [])
+    for step in range(1, STEPS + 1):
+        advance(step, [step + 2, step + 3], True)
+    both_ways(arrive, rows_out[5::2], [])
+    for step in range(1, STEPS + 1):
+        advance(step, [step, step + 1], True)
+    both_ways(leave, rows_out[0::2], rows_out[1::2])
+    for copy in (to_right, to_left, *[regrid(k) for k in range(1, n_lon)]):
         copy.wait_send()
+
+    @pl.when(comp == 0)
+    def _():
+        regrid(0).wait_send()
+
+    @pl.when(comp == 1)
+    def _():
+        handed.wait_send()
+
+    both_ways(leave, [corner_to_up, flux_to_up], [corner_to_down, flux_to_down])
     for store in stores:
         store.wait()
 
@@ -410,19 +509,22 @@
         scratch_shapes=[
             vmem((EXT + 1, LEV, LANES), F32),
             vmem((EXT + 1, LEV, LANES), F32),
+            vmem((EXT + 1, LEV, LANES), F32),
+            vmem((EXT + 1, LEV, LANES), F32),
+            vmem((ROWS, LEV, LANES), F32),
             vmem((8, LANES), F32),
             vmem((LEV, LEV), F32),
             vmem(diffusivity.shape, F32),
             vmem(weights.shape, F32),
             vmem((4, LINKS), jnp.int32),
-            vmem(land.shape, jnp.int32),
-            vmem(depth.shape, jnp.int32),
+            vmem((1, ROWS), jnp.int32),
+            vmem((1, ROWS), jnp.int32),
             vmem((LEV, 3 * LEV + 16), F32),
             vmem((LEV // 2 + 8, LANES), F32),
             vmem((LEV // 2 + 8, LANES), F32),
             vmem((LEV // 2 + 8, LANES), F32),
             vmem((n_lon, 16, LANES), F32),
-            vmem((n_lon, 16, LANES), F32),
+            vmem((2, n_lon, 16, LANES), F32),
             vmem((32, LANES), F32),
             vmem((32, LANES), F32),
             vmem((32, LANES), F32),
@@ -437,14 +539,18 @@
             dma((2,)),
             dma((2,)),
             dma((n_lon,)),
-            dma((n_lon,)),
+            dma((2, n_lon)),
             dma((2,)),
             dma((2,)),
             dma((2,)),
             dma((2,)),
+            vmem((11, LANES), F32),
+            vmem((11, LANES), F32),
+            dma,
+            dma,
         ],
         compiler_params=pltpu.CompilerParams(collective_id=0, has_side_effects=True),
-    )(state, mixing, diffusivity, weights, links, land, depth)
+    )(state, mixing, diffusivity, weights, links, land.reshape(1, ROWS), depth.reshape(1, ROWS))
 
 
 def solution(mesh):

time: 44.3 us -> 38.6 us (0.87)
  the two profiles are of different devices: /device:TPU:1 before, /device:TPU:14 now
where the time goes in v2:
time: 38.6 us; the launch traced here: 38.2 us
  Pallas kernels  36.5 us (95%)
  local copies, waits for them, and re-layouts  1.72 us (4%)
    pallas_call x1, Pallas kernels, on_device(): pl.pallas_call(functools.partial(kernel, n_lat, n_lon), out_shape=jax.Sha...  36.5 us
    unnamed x1, local copies, waits for them, and re-layouts  1.72 us

profile of v2, /device:TPU:14, one launch (start us, length us, event | category | flops | bytes accessed | tf_op | source)
XLA Modules:
  0.0 38.2 jit_solution(3292882811513461900)
XLA Ops:
  0.0 36.5 %shard_map.73 = f32[1,80,8,128]{3,2,1,0:T(8,128)} custom-call(f32[1,80,8,128]{3,2,1,0:T(8,128)} %state.1, f32[1,80,80]{2,1,0:T(8,128)} %mixing.1, f32[1,80]{1,0:T(1,128)} %diffusivity.1, f32[1,64]{1,0:T(1,128)} %weights.1, s32[1,1,1,4,32]{4,3,2,1,0:T(4,128)} %links.1, s32[1,8]{1,0:T(1,128)} %bitcast.2, s32[1,8]{1,0:T(1,128)} %bitcast.3), custom_call_target="tpu_custom_call" | custom-call | tf_op jit(solution)/shard_map/pallas_call | solution.py:504
  36.5 1.7 %copy.9 = f32[1,80,8,128]{3,2,1,0:T(8,128)} copy(f32[1,80,8,128]{3,2,1,0:T(8,128)} %shard_map.73) | data formatting | bytes 655360

commit v3 on v2

--- a/solution.py
+++ b/solution.py
@@ -53,7 +53,6 @@
     x1,
     x2,
     x3,
-    x4,
     surf,
     mixbuf,
     difbuf,
@@ -390,7 +389,7 @@
 
     first_lane, last_lane = lane == 0, lane == LANES - 1
     pad = jnp.zeros((16, LANES), BF16)
-    levels_at = (x0, x1, x2, x3, x4)
+    levels_at = (x0, x1, x2, x3, out)
     depths = {STEPS + r: depth_own[r : r + 1] for r in range(ROWS)}
     fluxes = {STEPS + r: flux_own[r : r + 1] for r in range(ROWS)}
 
@@ -417,8 +416,6 @@
         from_west = pltpu.roll(jnp.where(last_lane, z, centre), 1, 1)
         from_east = pltpu.roll(jnp.where(first_lane, z, centre), LANES - 1, 1)
         return operand(centre, src[e - 1] + src[e + 1] + from_west + from_east, e, step)
-
-    stores = []
 
     def advance(step, rows, merge):
         src, dst = levels_at[step - 1], levels_at[step]
@@ -435,9 +432,6 @@
                 if step == STEPS:
                     r = e - STEPS
                     dst[r] = new
-                    store = pltpu.make_async_copy(dst.at[r], out.at[0, :, r, :], load_sem.at[7 + r])
-                    store.start()
-                    stores.append(store)
                 else:
                     dst[e] = new
 
@@ -475,12 +469,9 @@
     top_flux = fluxes_up[...]
     fluxes[SIDE] = jnp.where(lane < 32, pltpu.roll(top_flux[0:1], 64, 1), flux_part)
     fluxes.update({1 + e: top_flux[5 + e : 6 + e] for e in range(3)})
-    both_ways(arrive, rows_out[1:4:2], [])
+    both_ways(arrive, rows_out[1::2], [])
     for step in range(1, STEPS + 1):
-        advance(step, [step + 2, step + 3], True)
-    both_ways(arrive, rows_out[5::2], [])
-    for step in range(1, STEPS + 1):
-        advance(step, [step, step + 1], True)
+        advance(step, [step, step + 1, step + 2, step + 3], True)
     both_ways(leave, rows_out[0::2], rows_out[1::2])
     for copy in (to_right, to_left, *[regrid(k) for k in range(1, n_lon)]):
         copy.wait_send()
@@ -494,24 +485,29 @@
         handed.wait_send()
 
     both_ways(leave, [corner_to_up, flux_to_up], [corner_to_down, flux_to_down])
-    for store in stores:
-        store.wait()
+
+
+def write_rows(rows, out, sem):
+    copies = [pltpu.make_async_copy(rows.at[r], out.at[0, :, r, :], sem.at[r]) for r in range(ROWS)]
+    for copy in copies:
+        copy.start()
+    for copy in copies:
+        copy.wait()
 
 
 def on_device(n_lat, n_lon, state, mixing, diffusivity, weights, links, land, depth):
     vmem = pltpu.VMEM
     dma = pltpu.SemaphoreType.DMA
-    return pl.pallas_call(
+    result = pl.pallas_call(
         functools.partial(kernel, n_lat, n_lon),
-        out_shape=jax.ShapeDtypeStruct(state.shape, F32),
+        out_shape=pltpu.VMEM((ROWS, LEV, LANES), F32),
         in_specs=[pl.BlockSpec(memory_space=pl.ANY)] * 7,
-        out_specs=pl.BlockSpec(memory_space=pl.ANY),
+        out_specs=pl.BlockSpec(memory_space=pltpu.VMEM),
         scratch_shapes=[
             vmem((EXT + 1, LEV, LANES), F32),
             vmem((EXT + 1, LEV, LANES), F32),
             vmem((EXT + 1, LEV, LANES), F32),
             vmem((EXT + 1, LEV, LANES), F32),
-            vmem((ROWS, LEV, LANES), F32),
             vmem((8, LANES), F32),
             vmem((LEV, LEV), F32),
             vmem(diffusivity.shape, F32),
@@ -551,6 +547,13 @@
         ],
         compiler_params=pltpu.CompilerParams(collective_id=0, has_side_effects=True),
     )(state, mixing, diffusivity, weights, links, land.reshape(1, ROWS), depth.reshape(1, ROWS))
+    return pl.pallas_call(
+        write_rows,
+        out_shape=jax.ShapeDtypeStruct(state.shape, F32),
+        in_specs=[pl.BlockSpec(memory_space=pltpu.VMEM)],
+        out_specs=pl.BlockSpec(memory_space=pl.ANY),
+        scratch_shapes=[dma((ROWS,))],
+    )(pltpu.with_memory_space_constraint(result, pltpu.VMEM))
 
 
 def solution(mesh):

time: 38.6 us -> 35.9 us (0.930)
  local copies, waits for them, and re-layouts: 1.72 us -> 0 us
  Pallas kernels: 36.5 us -> 35.5 us
    unnamed x1 -> x0, local copies, waits for them, and re-layouts: 1.72 us -> none
    pallas_call x1 -> x2, Pallas kernels: 36.5 us -> 35.5 us  [the longest x1 34.8 us: on_device(): pl.pallas_call(functools.partial(kernel, n_lat, n_lon), out_shape=pltpu.V...]
where the time goes in v3:
time: 35.9 us; the launch traced here: 35.5 us
  Pallas kernels  35.5 us (99%)
    pallas_call x1, Pallas kernels, on_device(): pl.pallas_call(functools.partial(kernel, n_lat, n_lon), out_shape=pltpu.V...  34.8 us
    pallas_call x1, Pallas kernels, on_device(): pl.pallas_call(write_rows, out_shape=jax.ShapeDtypeStruct(state.shape, F3...  0.78 us

profile of v3, /device:TPU:14, one launch (start us, length us, event | category | flops | bytes accessed | tf_op | source)
XLA Modules:
  0.0 35.5 jit_solution(6191747791759222316)
XLA Ops:
  0.0 34.8 %shard_map.73.rows = f32[8,80,128]{2,1,0:T(8,128)S(1)} custom-call(f32[1,80,8,128]{3,2,1,0:T(8,128)} %state.1, f32[1,80,80]{2,1,0:T(8,128)} %mixing.1, f32[1,80]{1,0:T(1,128)} %diffusivity.1, f32[1,64]{1,0:T(1,128)} %weights.1, s32[1,1,1,4,32]{4,3,2,1,0:T(4,128)} %links.1, s32[1,8]{1,0:T(1,128)} %bitcast.2, s32[1,8]{1,0:T(1,128)} %bitcast.3), custom_call_target="tpu_custom_call" | custom-call | tf_op jit(solution)/shard_map/pallas_call | solution.py:501
  34.8 0.8 %shard_map.74 = f32[1,80,8,128]{3,2,1,0:T(8,128)} custom-call(f32[8,80,128]{2,1,0:T(8,128)S(1)} %shard_map.73.rows), custom_call_target="tpu_custom_call" | custom-call | tf_op jit(solution)/shard_map/pallas_call | solution.py:550

commit v4 on v3

--- a/solution.py
+++ b/solution.py
@@ -291,7 +291,7 @@
     start = lambda copy: copy.start()
     arrive = lambda copy: copy.wait_recv()
     leave = lambda copy: copy.wait_send()
-    both_ways(start, rows_out[0:4:2], rows_out[1:4:2])
+    both_ways(start, rows_out[0::2], rows_out[1::2])
 
     loads[5].wait()
     loads[6].wait()
@@ -334,7 +334,7 @@
     corner_to_down = pltpu.make_async_remote_copy(
         corner_down, from_up, corner_send.at[1], corner_recv.at[1], device_id={"lat": down}, device_id_type=MESH
     )
-    both_ways(start, [corner_to_up, *rows_out[4::2]], [corner_to_down, *rows_out[5::2]])
+    both_ways(start, [corner_to_up], [corner_to_down])
 
     handed = pltpu.make_async_remote_copy(
         handing, given, hand_send, hand_recv, device_id={"comp": 0}, device_id_type=MESH

time: 35.9 us -> 35.5 us (0.989)
  no operation moved by 1% of the time
where the time goes in v4:
time: 35.5 us; the launch traced here: 35.4 us
  Pallas kernels  35.3 us (99%)
    pallas_call x1, Pallas kernels, on_device(): pl.pallas_call(functools.partial(kernel, n_lat, n_lon), out_shape=pltpu.V...  34.6 us
    pallas_call x1, Pallas kernels, on_device(): pl.pallas_call(write_rows, out_shape=jax.ShapeDtypeStruct(state.shape, F3...  0.78 us

profile of v4, /device:TPU:14, one launch (start us, length us, event | category | flops | bytes accessed | tf_op | source)
XLA Modules:
  0.0 35.4 jit_solution(13052136824904540691)
XLA Ops:
  0.0 34.6 %shard_map.73.rows = f32[8,80,128]{2,1,0:T(8,128)S(1)} custom-call(f32[1,80,8,128]{3,2,1,0:T(8,128)} %state.1, f32[1,80,80]{2,1,0:T(8,128)} %mixing.1, f32[1,80]{1,0:T(1,128)} %diffusivity.1, f32[1,64]{1,0:T(1,128)} %weights.1, s32[1,1,1,4,32]{4,3,2,1,0:T(4,128)} %links.1, s32[1,8]{1,0:T(1,128)} %bitcast.2, s32[1,8]{1,0:T(1,128)} %bitcast.3), custom_call_target="tpu_custom_call" | custom-call | tf_op jit(solution)/shard_map/pallas_call | solution.py:501
  34.6 0.8 %shard_map.74 = f32[1,80,8,128]{3,2,1,0:T(8,128)} custom-call(f32[8,80,128]{2,1,0:T(8,128)S(1)} %shard_map.73.rows), custom_call_target="tpu_custom_call" | custom-call | tf_op jit(solution)/shard_map/pallas_call | solution.py:550

commit v5 on v4

--- a/solution.py
+++ b/solution.py
@@ -291,7 +291,7 @@
     start = lambda copy: copy.start()
     arrive = lambda copy: copy.wait_recv()
     leave = lambda copy: copy.wait_send()
-    both_ways(start, rows_out[0::2], rows_out[1::2])
+    both_ways(start, rows_out[0:6:2], rows_out[1:6:2])
 
     loads[5].wait()
     loads[6].wait()
@@ -334,7 +334,7 @@
     corner_to_down = pltpu.make_async_remote_copy(
         corner_down, from_up, corner_send.at[1], corner_recv.at[1], device_id={"lat": down}, device_id_type=MESH
     )
-    both_ways(start, [corner_to_up], [corner_to_down])
+    both_ways(start, [corner_to_up, rows_out[6]], [corner_to_down, rows_out[7]])
 
     handed = pltpu.make_async_remote_copy(
         handing, given, hand_send, hand_recv, device_id={"comp": 0}, device_id_type=MESH

time: 35.5 us -> 35.5 us (level)
  no operation moved by 1% of the time
where the time goes in v5:
time: 35.5 us; the launch traced here: 35.3 us
  Pallas kernels  35.3 us (99%)
    pallas_call x1, Pallas kernels, on_device(): pl.pallas_call(functools.partial(kernel, n_lat, n_lon), out_shape=pltpu.V...  34.5 us
    pallas_call x1, Pallas kernels, on_device(): pl.pallas_call(write_rows, out_shape=jax.ShapeDtypeStruct(state.shape, F3...  0.78 us

profile of v5, /device:TPU:14, one launch (start us, length us, event | category | flops | bytes accessed | tf_op | source)
XLA Modules:
  0.0 35.3 jit_solution(9700622948176630938)
XLA Ops:
  0.0 34.5 %shard_map.73.rows = f32[8,80,128]{2,1,0:T(8,128)S(1)} custom-call(f32[1,80,8,128]{3,2,1,0:T(8,128)} %state.1, f32[1,80,80]{2,1,0:T(8,128)} %mixing.1, f32[1,80]{1,0:T(1,128)} %diffusivity.1, f32[1,64]{1,0:T(1,128)} %weights.1, s32[1,1,1,4,32]{4,3,2,1,0:T(4,128)} %links.1, s32[1,8]{1,0:T(1,128)} %bitcast.2, s32[1,8]{1,0:T(1,128)} %bitcast.3), custom_call_target="tpu_custom_call" | custom-call | tf_op jit(solution)/shard_map/pallas_call | solution.py:501
  34.5 0.8 %shard_map.74 = f32[1,80,8,128]{3,2,1,0:T(8,128)} custom-call(f32[8,80,128]{2,1,0:T(8,128)S(1)} %shard_map.73.rows), custom_call_target="tpu_custom_call" | custom-call | tf_op jit(solution)/shard_map/pallas_call | solution.py:550
